TPU v7x, 32 devices: a whole 2x2x4 slice. The times are simulated.
32 devices in a mesh: parts: 16 (over z, y, core), mp: 2 (over x).
Axes of the slice: x: 2, y: 2, z: 4, core: 2. Of those that a mesh axis runs over, the one named last changes fastest.
Arguments:
- feats: bfloat16 [2048, 1024], P('parts', 'mp'), may hold values from -6 to 6
- adj_local: bfloat16 [2048, 128], P('parts'), may hold values from -0.5 to 0.5
- adj_halo: bfloat16 [2048, 128], P('parts'), may hold values from -0.5 to 0.5
- w_graph: bfloat16 [1024, 1024], P(None, 'mp'), may hold values from -0.1875 to 0.1875
- w_query: bfloat16 [1024, 1024], P(None, 'mp'), may hold values from -0.1875 to 0.1875
- w_key: bfloat16 [1024, 1024], P(None, 'mp'), may hold values from -0.1875 to 0.1875
- w_value: bfloat16 [1024, 1024], P(None, 'mp'), may hold values from -0.1875 to 0.1875
- send_rows: int32 [16, 16, 8], P('parts'), may hold values from 0 to 127
- send_count: int32 [16, 16], P('parts'), may hold values from 0 to 8
- live: int32 [16], P('parts'), may hold values from 64 to 128
Outputs:
- attended: float32 [2048, 1024], P('parts', 'mp')
- key_summary: float32 [1024, 1024], P('mp')
All inputs are finite; a program needn't handle non-finite values.
Results may differ from a plain program's by a relative error of at most 0.0029.
The roundings to bfloat16 on the way count: a program that leaves them out, or rounds other values in their place, can miss the bound.
Values may be sent and summed in bfloat16 or wider, within the bound.
A program may use at most 64 MiB of HBM per device.

v0:
```python
import functools
import math

import jax
import jax.numpy as jnp
from jax import lax
from jax.experimental import pallas as pl
from jax.experimental.pallas import tpu as pltpu
from jax.sharding import PartitionSpec as P

MESH = pl.DeviceIdType.MESH
F32 = jnp.float32
BF16 = jnp.bfloat16


def plain(
    feats, adj_local, adj_halo, w_graph, w_query, w_key, w_value, send_rows, send_count, live
):
    row_count, col_count = feats.shape
    slot_count = send_rows.shape[2]
    picked = feats[send_rows[0]]
    slot_live = jnp.arange(slot_count, dtype=jnp.int32)[None, :] < send_count[0][:, None]
    outgoing = jnp.where(slot_live[:, :, None], picked, jnp.zeros((), jnp.bfloat16))
    incoming = lax.all_to_all(outgoing, "parts", split_axis=0, concat_axis=0, tiled=True)
    halo_rows = incoming.reshape(-1, col_count)
    summed = jnp.dot(adj_local, feats, preferred_element_type=jnp.float32)
    summed = summed + jnp.dot(adj_halo, halo_rows, preferred_element_type=jnp.float32)
    convolved = summed.astype(jnp.bfloat16)
    out_cols = w_graph.shape[1]
    empty = jnp.zeros((row_count, out_cols), jnp.float32)
    weight_rows = w_graph
    projected = jnp.dot(
        lax.all_gather(convolved, "mp", axis=1, tiled=True),
        weight_rows,
        preferred_element_type=jnp.float32,
    )
    hidden = jax.nn.gelu(projected, approximate=False).astype(jnp.bfloat16)
    totals = (empty, empty, empty)
    portion = lax.all_gather(hidden, "mp", axis=1, tiled=True)
    outputs = []
    for running, weight in zip(totals, (w_query, w_key, w_value)):
        weight_rows = weight
        outputs.append(jnp.dot(portion, weight_rows, preferred_element_type=jnp.float32))
    queries, keys_raw, values_wide = tuple(outputs)
    live_mask = jnp.arange(row_count, dtype=jnp.int32)[:, None] < live[0]
    query_feat = jnp.where(live_mask, jax.nn.elu(queries) + 1.0, 0.0).astype(jnp.bfloat16)
    key_feat = jnp.where(live_mask, jax.nn.elu(keys_raw) + 1.0, 0.0).astype(jnp.bfloat16)
    values = values_wide.astype(jnp.bfloat16)
    key_values = lax.dot_general(
        key_feat,
        lax.all_gather(values, "mp", axis=1, tiled=True),
        (((0,), (0,)), ((), ())),
        preferred_element_type=jnp.float32,
    )
    query_wide = query_feat.astype(jnp.float32)
    key_wide = key_feat.astype(jnp.float32)
    key_total = jnp.sum(key_wide, axis=0)
    sq_pair = jnp.stack([jnp.sum(query_wide * query_wide), jnp.sum(key_wide * key_wide)])
    key_values, key_total, sq_pair = lax.psum((key_values, key_total, sq_pair), "parts")
    key_summary = key_values / math.sqrt(lax.axis_size("parts") * row_count)
    numer_part = jnp.dot(
        query_feat, key_values.astype(jnp.bfloat16), preferred_element_type=jnp.float32
    )
    denom_part = jnp.dot(query_wide, key_total, precision=lax.Precision.HIGHEST)
    numerator = lax.psum_scatter(
        numer_part.astype(jnp.bfloat16), "mp", scatter_dimension=1, tiled=True
    ).astype(jnp.float32)
    denominator, sq_pair = lax.psum((denom_part, sq_pair), "mp")
    inverse = lax.rsqrt(sq_pair[0]) * lax.rsqrt(sq_pair[1])
    result = (values.astype(jnp.float32) + numerator * inverse) / (1.0 + denominator * inverse)[
        :, None
    ]
    return (jnp.where(live_mask, result, 0.0), key_summary)


def dot(a, b):
    return jnp.dot(a, b, preferred_element_type=F32)


def kernel(
    n,
    nz,
    feats_in,
    adj_local_in,
    adj_halo_in,
    send_rows_in,
    send_count_in,
    live,
    wg,
    wq,
    wk,
    wv,
    out,
    kv_out,
    feats,
    adj_local,
    adj_halo,
    send_rows,
    send_count,
    wbuf,
    outgoing,
    incoming,
    conv,
    hid,
    val,
    query,
    key_t,
    part,
    send1,
    recv1,
    acc2,
    send2,
    recv2,
    send3,
    recv3,
    kvb,
    stat,
    den,
    nsend,
    nrecv,
    isem,
    wsem,
    osem,
    halo_s,
    halo_r,
    mp_s,
    mp_r,
    s1_s,
    s1_r,
    s2_s,
    s2_r,
    s3_s,
    s3_r,
    gz_s,
    gz_r,
    gy_s,
    gy_r,
    gc_s,
    gc_r,
    st_s,
    st_r,
):
    p = lax.axis_index("parts")
    m = lax.axis_index("mp")
    c, y, z = p % 2, (p // 2) % 2, p // 4
    other = 1 - m
    core_peer = p + 1 - 2 * c
    y_peer = p + 2 - 4 * y
    rows, cols = feats.shape
    slots = outgoing.shape[1]
    half, quarter, piece = cols // 2, cols // 4, cols // n
    sent = []

    def send(src, dst, s_sem, r_sem, device):
        copy = pltpu.make_async_remote_copy(
            src_ref=src,
            dst_ref=dst,
            send_sem=s_sem,
            recv_sem=r_sem,
            device_id=device,
            device_id_type=MESH,
        )
        copy.start()
        sent.append(copy)
        return copy

    inputs = []
    for i, (source, place) in enumerate(
        (
            (send_rows_in, send_rows),
            (send_count_in, send_count),
            (feats_in, feats),
            (adj_local_in, adj_local),
            (adj_halo_in, adj_halo),
        )
    ):
        load = pltpu.make_async_copy(source, place, isem.at[i])
        load.start()
        inputs.append(load)
    loads = []
    for i, w in enumerate((wg, wv, wk, wq)):
        load = pltpu.make_async_copy(w, wbuf.at[i], wsem.at[i])
        load.start()
        loads.append(load)

    barrier = pltpu.get_barrier_semaphore()
    for d in range(1, n):
        pl.semaphore_signal(
            barrier, inc=1, device_id={"parts": lax.rem(p + d, n)}, device_id_type=MESH
        )
    pl.semaphore_signal(barrier, inc=1, device_id={"mp": other}, device_id_type=MESH)

    for load in inputs:
        load.wait()

    total = n * slots
    owner = lax.broadcasted_iota(jnp.int32, (total, n), 0) // slots
    is_owner = owner == lax.broadcasted_iota(jnp.int32, (total, n), 1)
    spot = lax.broadcasted_iota(jnp.int32, (total, slots), 0) % slots
    is_spot = spot == lax.broadcasted_iota(jnp.int32, (total, slots), 1)
    spread = lax.dot_general(
        is_owner.astype(F32),
        send_rows[...].astype(F32),
        (((1,), (1,)), ((), ())),
        precision=lax.Precision.HIGHEST,
        preferred_element_type=F32,
    )
    index = jnp.sum(jnp.where(is_spot, spread, 0.0), axis=1, keepdims=True)
    count = jnp.sum(
        jnp.where(is_owner, send_count[...].astype(F32), 0.0), axis=1, keepdims=True
    )
    slot_id = jnp.sum(
        jnp.where(is_spot, lax.broadcasted_iota(jnp.int32, (total, slots), 1), 0).astype(F32),
        axis=1,
        keepdims=True,
    )
    index = jnp.where(slot_id < count, index, -1.0)
    node = lax.broadcasted_iota(jnp.int32, (total, rows), 1).astype(F32)
    pick = jnp.where(index == node, 1.0, 0.0).astype(BF16)
    outgoing[...] = dot(pick, feats[...]).reshape(n, slots, cols).astype(BF16)

    pl.semaphore_wait(barrier, n)
    halo = []
    for d in range(1, n):
        to = lax.rem(p + d, n)
        halo.append(
            send(outgoing.at[to], incoming.at[p], halo_s.at[d], halo_r.at[d], {"parts": to})
        )
    incoming[p] = outgoing[p]
    local_sum = dot(adj_local[...], feats[...])
    for copy in halo:
        copy.wait_recv()
    arrived = incoming[...].astype(F32).reshape(total, cols).astype(BF16)
    conv[m] = (local_sum + dot(adj_halo[...], arrived)).astype(BF16)
    swap = send(conv.at[m], conv.at[m], mp_s.at[0], mp_r.at[0], {"mp": other})
    mine = pl.ds(pl.multiple_of(m * cols, cols), cols)
    theirs = pl.ds(pl.multiple_of(other * cols, cols), cols)
    loads[0].wait()
    projected = dot(conv[m], wbuf[0, mine, :])
    swap.wait_recv()
    projected = projected + dot(conv[other], wbuf[0, theirs, :])
    hid[m] = (0.5 * projected * (1.0 + lax.erf(projected * math.sqrt(0.5)))).astype(BF16)
    swap = send(hid.at[m], hid.at[m], mp_s.at[1], mp_r.at[1], {"mp": other})
    for load in loads[1:]:
        load.wait()
    own = hid[m]
    raw_v = dot(own, wbuf[1, mine, :])
    raw_k = dot(own, wbuf[2, mine, :])
    raw_q = dot(own, wbuf[3, mine, :])
    swap.wait_recv()
    rest = hid[other]
    val[m] = (raw_v + dot(rest, wbuf[1, theirs, :])).astype(BF16)
    swap = send(val.at[m], val.at[m], mp_s.at[2], mp_r.at[2], {"mp": other})
    live_mask = lax.broadcasted_iota(jnp.int32, (rows, 1), 0) < live[0]

    def feature(x):
        x = jnp.where(x > 0.0, x + 1.0, jnp.exp(jnp.minimum(x, 0.0)))
        return jnp.where(live_mask, x, 0.0).astype(BF16)

    key_feat = feature(raw_k + dot(rest, wbuf[2, theirs, :]))
    key_wide = key_feat.astype(F32)
    key_t[...] = key_wide.T.astype(BF16)

    keep1 = pl.ds(pl.multiple_of(c * half, half), half)
    give1 = pl.ds(pl.multiple_of((1 - c) * half, half), half)
    keep2 = pl.ds(pl.multiple_of(y * quarter, quarter), quarter)
    give2 = pl.ds(pl.multiple_of((1 - y) * quarter, quarter), quarter)
    step1 = []

    def start1(g, column):
        send1[g] = dot(key_t[give1, :], val[column]).astype(BF16)
        step1.append(
            send(send1.at[g], recv1.at[g], s1_s.at[g], s1_r.at[g], {"parts": core_peer})
        )
        part[g] = dot(key_t[keep1, :], val[column])

    start1(0, m)
    query[...] = feature(raw_q + dot(rest, wbuf[3, theirs, :]))
    query_wide = query[...].astype(F32)
    lane = lax.broadcasted_iota(jnp.int32, (1, 128), 1)
    query_sq = jnp.sum(jnp.sum(query_wide * query_wide, axis=0, keepdims=True), axis=1, keepdims=True)
    key_sq = jnp.sum(jnp.sum(key_wide * key_wide, axis=0, keepdims=True), axis=1, keepdims=True)
    stat[0, :, :cols] = jnp.sum(key_wide, axis=0, keepdims=True)
    stat[0, :, cols:] = jnp.where(lane == 0, query_sq, jnp.where(lane == 1, key_sq, 0.0))
    swap.wait_recv()
    start1(1, other)
    stats = []
    for d in range(1, n):
        stats.append(
            send(stat.at[0], stat.at[d], st_s.at[d], st_r.at[d], {"parts": lax.rem(p + d, n)})
        )
    step2, step3 = {}, {}
    order = ((1, other), (0, m))
    for g, _ in order:
        step1[g].wait_recv()
        send2[g] = (
            part[g, give2, :]
            + recv1[g, give2, :].astype(F32)
        ).astype(BF16)
        step2[g] = send(
            send2.at[g], recv2.at[g], s2_s.at[g], s2_r.at[g], {"parts": y_peer}
        )
        acc2[g] = part[g, keep2, :] + recv1[g, keep2, :].astype(F32)
    for g, _ in order:
        step2[g].wait_recv()
        acc2[g] = acc2[g] + recv2[g].astype(F32)
        send3[g] = acc2[g].astype(BF16)
        for d in range(1, nz):
            to = lax.rem(z + d, nz)
            step3[g, d] = send(
                send3.at[g, pl.ds(pl.multiple_of(to * piece, piece), piece), :],
                recv3.at[g, d],
                s3_s.at[g, d],
                s3_r.at[g, d],
                {"parts": to * 4 + p % 4},
            )

    def block(column, yy, zz):
        first = c * half + yy * quarter + zz * piece
        return kvb.at[column, pl.ds(pl.multiple_of(first, piece), piece), :]

    gather_z, gather_y, gather_c = {}, {}, {}

    def to_core(g, place, i):
        gather_c[g, i] = send(
            place, place, gc_s.at[g, i], gc_r.at[g, i], {"parts": core_peer}
        )

    def pass_on(g, column, d):
        place = block(column, y, lax.rem(z + nz - d, nz))
        gather_y[g, d] = send(place, place, gy_s.at[g, d], gy_r.at[g, d], {"parts": y_peer})
        to_core(g, place, d)

    for g, column in order:
        final = acc2[g, pl.ds(pl.multiple_of(z * piece, piece), piece), :]
        for d in range(1, nz):
            step3[g, d].wait_recv()
            final = final + recv3[g, d].astype(F32)
        place = block(column, y, z)
        place[...] = final.astype(BF16)
        for d in range(1, nz):
            gather_z[g, d] = send(
                place,
                place,
                gz_s.at[g, d],
                gz_r.at[g, d],
                {"parts": lax.rem(z + d, nz) * 4 + p % 4},
            )
        pass_on(g, column, 0)

    for copy in stats:
        copy.wait_recv()
    sums = stat[0]
    for d in range(1, n):
        sums = sums + stat[d]
    den[m, :rows, :] = jnp.broadcast_to(
        jnp.sum(query_wide * sums[:, :cols], axis=1, keepdims=True), (rows, 128)
    )
    den[m, rows:, :] = jnp.broadcast_to(sums[:, cols:], (8, 128))
    den_swap = send(den.at[m], den.at[m], mp_s.at[3], mp_r.at[3], {"mp": other})

    for g, column in order:
        for d in range(1, nz):
            gather_z[g, d].wait_recv()
            pass_on(g, column, d)

    numerators = []
    for g, column in order:
        for d in range(nz):
            gather_y[g, d].wait_recv()
            to_core(g, block(column, 1 - y, lax.rem(z + nz - d, nz)), nz + d)
        for i in range(2 * nz):
            gather_c[g, i].wait_recv()
        numerators.append(dot(query[...], kvb[column]))
        if g == 1:
            nsend[...] = numerators[0].astype(BF16)
            swap = send(nsend, nrecv, mp_s.at[4], mp_r.at[4], {"mp": other})
    numerator = numerators[1]
    stores = []
    for g in range(2):
        store = pltpu.make_async_copy(kvb.at[g], kv_out.at[:, pl.ds(g * cols, cols)], osem.at[g])
        store.start()
        stores.append(store)
    den_swap.wait_recv()
    square = den[0, rows : rows + 1, :] + den[1, rows : rows + 1, :]
    query_sq = jnp.sum(jnp.where(lane == 0, square, 0.0), axis=1, keepdims=True)
    key_sq = jnp.sum(jnp.where(lane == 1, square, 0.0), axis=1, keepdims=True)
    inverse = lax.rsqrt(query_sq) * lax.rsqrt(key_sq)
    denominator = den[0, :rows, 0:1] + den[1, :rows, 0:1]
    scale = 1.0 + denominator * inverse
    swap.wait_recv()
    numerator = numerator + nrecv[...].astype(F32)
    result = (val[m].astype(F32) + numerator * inverse) / scale
    out[...] = jnp.where(live_mask, result, 0.0)
    for store in stores:
        store.wait()
    for copy in sent:
        copy.wait_send()


def fused(
    feats, adj_local, adj_halo, w_graph, w_query, w_key, w_value, send_rows, send_count, live
):
    n = lax.axis_size("parts")
    nz = n // 4
    rows, cols = feats.shape
    slots = send_rows.shape[2]
    depth = w_graph.shape[0]
    half, quarter, piece = cols // 2, cols // 4, cols // n
    vmem = pl.BlockSpec(memory_space=pltpu.VMEM)
    hbm = pl.BlockSpec(memory_space=pltpu.HBM)
    dma = pltpu.SemaphoreType.DMA
    place = functools.partial(pltpu.with_memory_space_constraint, memory_space=pltpu.HBM)
    out, kv = pl.pallas_call(
        functools.partial(kernel, n, nz),
        out_shape=(
            jax.ShapeDtypeStruct((rows, cols), F32),
            jax.ShapeDtypeStruct((cols, depth), BF16),
        ),
        in_specs=[hbm] * 5 + [pl.BlockSpec(memory_space=pltpu.SMEM)] + [hbm] * 4,
        out_specs=(vmem, pl.BlockSpec(memory_space=pl.ANY)),
        scratch_shapes=[
            pltpu.VMEM(feats.shape, BF16),
            pltpu.VMEM(adj_local.shape, BF16),
            pltpu.VMEM(adj_halo.shape, BF16),
            pltpu.VMEM((slots, n), jnp.int32),
            pltpu.VMEM((1, n), jnp.int32),
            pltpu.VMEM((4, depth, cols), BF16),
            pltpu.VMEM((n, slots, cols), BF16),
            pltpu.VMEM((n, slots, cols), BF16),
            pltpu.VMEM((2, rows, cols), BF16),
            pltpu.VMEM((2, rows, cols), BF16),
            pltpu.VMEM((2, rows, cols), BF16),
            pltpu.VMEM((rows, cols), BF16),
            pltpu.VMEM((cols, rows), BF16),
            pltpu.VMEM((2, half, cols), F32),
            pltpu.VMEM((2, half, cols), BF16),
            pltpu.VMEM((2, half, cols), BF16),
            pltpu.VMEM((2, quarter, cols), F32),
            pltpu.VMEM((2, quarter, cols), BF16),
            pltpu.VMEM((2, quarter, cols), BF16),
            pltpu.VMEM((2, quarter, cols), BF16),
            pltpu.VMEM((2, nz, piece, cols), BF16),
            pltpu.VMEM((2, cols, cols), BF16),
            pltpu.VMEM((n, 1, cols + 128), F32),
            pltpu.VMEM((2, rows + 8, 128), F32),
            pltpu.VMEM((rows, cols), BF16),
            pltpu.VMEM((rows, cols), BF16),
            dma((5,)),
            dma((4,)),
            dma((2,)),
            dma((n,)),
            dma((n,)),
            dma((5,)),
            dma((5,)),
            dma((2,)),
            dma((2,)),
            dma((2,)),
            dma((2,)),
            dma((2, nz)),
            dma((2, nz)),
            dma((2, nz)),
            dma((2, nz)),
            dma((2, nz)),
            dma((2, nz)),
            dma((2, 2 * nz)),
            dma((2, 2 * nz)),
            dma((n,)),
            dma((n,)),
        ],
        compiler_params=pltpu.CompilerParams(
            collective_id=0, has_side_effects=True, vmem_limit_bytes=24 * 1024 * 1024
        ),
    )(
        *(place(a) for a in (feats, adj_local, adj_halo, send_rows[0].T, send_count)),
        live,
        *(place(w) for w in (w_graph, w_query, w_key, w_value)),
    )
    return out, kv.astype(F32) / math.sqrt(n * rows)


def local(*args):
    n = lax.axis_size("parts")
    rows, cols = args[0].shape
    slots = args[7].shape[2]
    fits = (
        lax.axis_size("mp") == 2
        and n % 4 == 0
        and cols % (16 * n) == 0
        and rows % 16 == 0
        and (n * slots) % 16 == 0
        and slots % 8 == 0
    )
    return fused(*args) if fits else plain(*args)


def solution(mesh):
    return jax.shard_map(
        local,
        mesh=mesh,
        in_specs=(
            P("parts", "mp"),
            P("parts", None),
            P("parts", None),
            P(None, "mp"),
            P(None, "mp"),
            P(None, "mp"),
            P(None, "mp"),
            P("parts", None, None),
            P("parts", None),
            P("parts"),
        ),
        out_specs=(P("parts", "mp"), P("mp", None)),
        check_vma=False,
    )
```

profile of v0, /device:TPU:0, one launch (start us, length us, event | category | flops | bytes accessed | tf_op | source)
XLA Modules:
  0.0 55.6 jit_solution(13114961199826640376)
XLA Ops:
  1.3 52.0 %shard_map.113 = (f32[128,512]{1,0:T(8,128)S(1)}, bf16[512,1024]{1,0:T(8,128)(2,1)S(1)}) custom-call(bf16[128,512]{1,0:T(8,128)(2,1)} %feats_in.1, bf16[128,128]{1,0:T(8,128)(2,1)} %adj_local_in.1, bf16[128,128]{1,0:T(8,128)(2,1)} %adj_halo_in.1, s32[8,16]{1,0:T(8,128)} %bitcast.3, s32[1,16]{1,0:T(1,128)} %send_count_in.1, s32[1]{0:T(128)S(6)} %copy.13.live, ...), custom_call_target="tpu_custom_call" | custom-call | tf_op jit(solution)/shard_map/pallas_call | solution.py:414
  53.3 1.6 %convert_multiply_fusion = f32[512,1024]{1,0:T(8,128)} fusion(bf16[512,1024]{1,0:T(8,128)(2,1)S(1)} %get-tuple-element.5), kind=kLoop, calls=%fused_computation | loop fusion | flops 1048576 | bytes 3145728 | tf_op jit(solution)/shard_map/div | solution.py:479
  54.9 0.7 %copy.14 = f32[128,512]{1,0:T(8,128)} copy(f32[128,512]{1,0:T(8,128)S(1)} %get-tuple-element.8) | data formatting | bytes 524288
where the time goes:
time: 55.8 us; the launch traced here: 55.6 us
  Pallas kernels  52 us (93%)
  other arithmetic  1.6 us (3%)
  between operations  1.29 us (2%)
  local copies, waits for them, and re-layouts  0.7 us (1%)
    pallas_call x1, Pallas kernels, fused(): pl.pallas_call(functools.partial(kernel, n, nz), out_shape=(jax.ShapeDtyp...  52 us
    div x1, other arithmetic, fused(): return (out, kv.astype(F32) / math.sqrt(n * rows))  1.6 us

commit v1 on v0

v1 whole, which is shorter than its diff:
```python
import functools
import math

import jax
import jax.numpy as jnp
from jax import lax
from jax.experimental import pallas as pl
from jax.experimental.pallas import tpu as pltpu
from jax.sharding import PartitionSpec as P

MESH = pl.DeviceIdType.MESH
F32 = jnp.float32
BF16 = jnp.bfloat16


def plain(
    feats, adj_local, adj_halo, w_graph, w_query, w_key, w_value, send_rows, send_count, live
):
    row_count, col_count = feats.shape
    slot_count = send_rows.shape[2]
    picked = feats[send_rows[0]]
    slot_live = jnp.arange(slot_count, dtype=jnp.int32)[None, :] < send_count[0][:, None]
    outgoing = jnp.where(slot_live[:, :, None], picked, jnp.zeros((), jnp.bfloat16))
    incoming = lax.all_to_all(outgoing, "parts", split_axis=0, concat_axis=0, tiled=True)
    halo_rows = incoming.reshape(-1, col_count)
    summed = jnp.dot(adj_local, feats, preferred_element_type=jnp.float32)
    summed = summed + jnp.dot(adj_halo, halo_rows, preferred_element_type=jnp.float32)
    convolved = summed.astype(jnp.bfloat16)
    out_cols = w_graph.shape[1]
    empty = jnp.zeros((row_count, out_cols), jnp.float32)
    weight_rows = w_graph
    projected = jnp.dot(
        lax.all_gather(convolved, "mp", axis=1, tiled=True),
        weight_rows,
        preferred_element_type=jnp.float32,
    )
    hidden = jax.nn.gelu(projected, approximate=False).astype(jnp.bfloat16)
    totals = (empty, empty, empty)
    portion = lax.all_gather(hidden, "mp", axis=1, tiled=True)
    outputs = []
    for running, weight in zip(totals, (w_query, w_key, w_value)):
        weight_rows = weight
        outputs.append(jnp.dot(portion, weight_rows, preferred_element_type=jnp.float32))
    queries, keys_raw, values_wide = tuple(outputs)
    live_mask = jnp.arange(row_count, dtype=jnp.int32)[:, None] < live[0]
    query_feat = jnp.where(live_mask, jax.nn.elu(queries) + 1.0, 0.0).astype(jnp.bfloat16)
    key_feat = jnp.where(live_mask, jax.nn.elu(keys_raw) + 1.0, 0.0).astype(jnp.bfloat16)
    values = values_wide.astype(jnp.bfloat16)
    key_values = lax.dot_general(
        key_feat,
        lax.all_gather(values, "mp", axis=1, tiled=True),
        (((0,), (0,)), ((), ())),
        preferred_element_type=jnp.float32,
    )
    query_wide = query_feat.astype(jnp.float32)
    key_wide = key_feat.astype(jnp.float32)
    key_total = jnp.sum(key_wide, axis=0)
    sq_pair = jnp.stack([jnp.sum(query_wide * query_wide), jnp.sum(key_wide * key_wide)])
    key_values, key_total, sq_pair = lax.psum((key_values, key_total, sq_pair), "parts")
    key_summary = key_values / math.sqrt(lax.axis_size("parts") * row_count)
    numer_part = jnp.dot(
        query_feat, key_values.astype(jnp.bfloat16), preferred_element_type=jnp.float32
    )
    denom_part = jnp.dot(query_wide, key_total, precision=lax.Precision.HIGHEST)
    numerator = lax.psum_scatter(
        numer_part.astype(jnp.bfloat16), "mp", scatter_dimension=1, tiled=True
    ).astype(jnp.float32)
    denominator, sq_pair = lax.psum((denom_part, sq_pair), "mp")
    inverse = lax.rsqrt(sq_pair[0]) * lax.rsqrt(sq_pair[1])
    result = (values.astype(jnp.float32) + numerator * inverse) / (1.0 + denominator * inverse)[
        :, None
    ]
    return (jnp.where(live_mask, result, 0.0), key_summary)


def dot(a, b):
    return jnp.dot(a, b, preferred_element_type=F32)


def kernel(
    n,
    chunks,
    feats_in,
    adj_local_in,
    adj_halo_in,
    send_rows_in,
    send_count_in,
    live,
    wg,
    wq,
    wk,
    wv,
    out,
    kv_out,
    feats,
    adj_local,
    adj_halo,
    send_rows,
    send_count,
    wbuf,
    outgoing,
    incoming,
    conv,
    hid,
    val,
    query,
    keyb,
    keyx,
    queryb,
    queryx,
    tbuf,
    ysend,
    yrecv,
    acc,
    zsend,
    zrecv,
    kvl,
    kvs,
    kvx,
    kvxs,
    nsend,
    nrecv,
    stat,
    den,
    isem,
    wsem,
    osem,
    feat_sem,
    halo_s,
    halo_r,
    fwd_s,
    fwd_r,
    hid_sem,
    key_s,
    key_r,
    query_s,
    query_r,
    val_sem,
    num_s,
    num_r,
    y_s,
    y_r,
    z_s,
    z_r,
    g_s,
    g_r,
    gy_s,
    gy_r,
    gx_s,
    gx_r,
    gc_s,
    gc_r,
    gd_s,
    gd_r,
    st_s,
    st_r,
    den_sem,
):
    p = lax.axis_index("parts")
    m = lax.axis_index("mp")
    c, y, z = p % 2, (p // 2) % 2, p // 4
    other = 1 - m
    sibling = p + 1 - 2 * c
    y_peer = p + 2 - 4 * y
    rows, cols = feats.shape[1:]
    slots = outgoing.shape[1]
    total = n * slots
    half, piece = cols // 2, zrecv.shape[2]
    width = zrecv.shape[3]
    groups = cols // width

    z_near = z + 1 - 2 * (z % 2)
    z_far = lax.rem(z + 2, 4)
    z_mirror = 3 - z
    edge = jnp.logical_or(z == 0, z == 3)
    inner = jnp.logical_not(edge)

    def spot_of(yy, zz):
        return pl.ds(pl.multiple_of((yy * 4 + zz) * piece, piece), piece)

    def make(src, dst, s_sem, r_sem, device):
        return pltpu.make_async_remote_copy(
            src_ref=src,
            dst_ref=dst,
            send_sem=s_sem,
            recv_sem=r_sem,
            device_id=device,
            device_id_type=MESH,
        )

    def send(src, dst, s_sem, r_sem, device):
        copy = make(src, dst, s_sem, r_sem, device)
        copy.start()
        return copy

    def wait_for(like, sem):
        pltpu.make_async_copy(like, like, sem).wait()

    inputs = []
    for i, (source, place) in enumerate(
        (
            (send_rows_in, send_rows),
            (send_count_in, send_count),
            (feats_in, feats.at[m]),
            (adj_local_in, adj_local),
            (adj_halo_in, adj_halo),
        )
    ):
        load = pltpu.make_async_copy(source, place, isem.at[i])
        load.start()
        inputs.append(load)
    loads = []
    for i, w in enumerate((wg, wk, wv, wq)):
        load = pltpu.make_async_copy(w, wbuf.at[i], wsem.at[i])
        load.start()
        loads.append(load)

    barrier = pltpu.get_barrier_semaphore()
    for d in range(1, n):
        pl.semaphore_signal(
            barrier, inc=1, device_id={"parts": lax.rem(p + d, n)}, device_id_type=MESH
        )
    for to in (p, sibling, y_peer):
        pl.semaphore_signal(
            barrier, inc=1, device_id={"parts": to, "mp": other}, device_id_type=MESH
        )

    for load in inputs:
        load.wait()

    owner = lax.broadcasted_iota(jnp.int32, (total, n), 0) // slots
    is_owner = owner == lax.broadcasted_iota(jnp.int32, (total, n), 1)
    spot = lax.broadcasted_iota(jnp.int32, (total, slots), 0) % slots
    is_spot = spot == lax.broadcasted_iota(jnp.int32, (total, slots), 1)
    spread = lax.dot_general(
        is_owner.astype(F32),
        send_rows[...].astype(F32),
        (((1,), (1,)), ((), ())),
        precision=lax.Precision.HIGHEST,
        preferred_element_type=F32,
    )
    index = jnp.sum(jnp.where(is_spot, spread, 0.0), axis=1, keepdims=True)
    count = jnp.sum(
        jnp.where(is_owner, send_count[...].astype(F32), 0.0), axis=1, keepdims=True
    )
    slot_id = jnp.sum(
        jnp.where(is_spot, lax.broadcasted_iota(jnp.int32, (total, slots), 1), 0).astype(F32),
        axis=1,
        keepdims=True,
    )
    index = jnp.where(slot_id < count, index, -1.0)
    node = lax.broadcasted_iota(jnp.int32, (total, rows), 1).astype(F32)
    pick = jnp.where(index == node, 1.0, 0.0).astype(BF16)
    outgoing[...] = dot(pick, feats[m]).reshape(n, slots, cols).astype(BF16)

    def partner(k):
        kz, ky, kc = k // 4, (k // 2) % 2, k % 2
        zz = (z, z_near, z_far, z_mirror)[kz]
        yy = 1 - y if ky else y
        cc = 1 - c if kc else c
        return zz * 4 + yy * 2 + cc

    pl.semaphore_wait(barrier, n + 2)
    for k in (*range(12, n), *range(8, 12), *range(4, 8), *range(1, 4)):
        to = partner(k)
        send(outgoing.at[to], incoming.at[m, p], halo_s, halo_r.at[k // 4], {"parts": to})
    swap_feats = send(feats.at[m], feats.at[m], feat_sem.at[0], feat_sem.at[1], {"mp": other})
    send(outgoing.at[p], incoming.at[m, p], fwd_s, fwd_r, {"mp": other})
    incoming[m, p] = outgoing[p]
    local_mine = dot(adj_local[...], feats[m])
    for kz in range(4):
        members = range(max(1, 4 * kz), 4 * kz + 4)
        wait_for(outgoing.at[pl.ds(0, len(members))], halo_r.at[kz])
        for k in members:
            block = incoming.at[m, partner(k)]
            send(block, block, fwd_s, fwd_r, {"mp": other})

    def convolve(side, local_sum):
        arrived = incoming[side].astype(F32).reshape(total, cols).astype(BF16)
        conv[side] = (local_sum + dot(adj_halo[...], arrived)).astype(BF16)

    mine = pl.ds(pl.multiple_of(m * cols, cols), cols)
    theirs = pl.ds(pl.multiple_of(other * cols, cols), cols)
    convolve(m, local_mine)
    loads[0].wait()
    projected = dot(conv[m], wbuf[0, mine, :])
    swap_feats.wait_recv()
    local_theirs = dot(adj_local[...], feats[other])
    wait_for(outgoing, fwd_r)
    convolve(other, local_theirs)
    projected = projected + dot(conv[other], wbuf[0, theirs, :])
    hid[m] = (0.5 * projected * (1.0 + lax.erf(projected * math.sqrt(0.5)))).astype(BF16)
    swap = send(hid.at[m], hid.at[m], hid_sem.at[0], hid_sem.at[1], {"mp": other})
    for load in loads[1:]:
        load.wait()
    own = hid[m]
    raw_k = dot(own, wbuf[1, mine, :])
    raw_v = dot(own, wbuf[2, mine, :])
    raw_q = dot(own, wbuf[3, mine, :])
    live_mask = lax.broadcasted_iota(jnp.int32, (rows, 1), 0) < live[0]

    def feature(x):
        x = jnp.where(x > 0.0, x + 1.0, jnp.exp(jnp.minimum(x, 0.0)))
        return jnp.where(live_mask, x, 0.0).astype(BF16)

    def spread_blocks(blocks, place, s_sems, r_sems):
        away = blocks.at[1 - c]
        return [
            send(blocks.at[c], place.at[1, c], s_sems.at[0], r_sems.at[0], {"mp": other}),
            send(
                away,
                place.at[1, c],
                s_sems.at[1],
                r_sems.at[1],
                {"parts": sibling, "mp": other},
            ),
            send(away, place.at[0, c], s_sems.at[2], r_sems.at[2], {"parts": sibling}),
        ]

    swap.wait_recv()
    rest = hid[other]
    key_feat = feature(raw_k + dot(rest, wbuf[1, theirs, :]))
    key_wide = key_feat.astype(F32)
    key_t = key_wide.T.astype(BF16)
    for b in range(2):
        keyb[b] = key_t[b * half : (b + 1) * half]
    keys = spread_blocks(keyb, keyx, key_s, key_r)
    val[c] = (raw_v + dot(rest, wbuf[2, theirs, :])).astype(BF16)
    values = send(val.at[c], val.at[c], val_sem.at[0], val_sem.at[1], {"parts": sibling})
    query_feat = feature(raw_q + dot(rest, wbuf[3, theirs, :]))
    query[...] = query_feat
    for b in range(2):
        queryb[b] = query_feat[:, b * half : (b + 1) * half]
    query_wide = query_feat.astype(F32)
    lane = lax.broadcasted_iota(jnp.int32, (1, 128), 1)
    query_sq = jnp.sum(jnp.sum(query_wide * query_wide, axis=0, keepdims=True), axis=1, keepdims=True)
    key_sq = jnp.sum(jnp.sum(key_wide * key_wide, axis=0, keepdims=True), axis=1, keepdims=True)
    stat[0, :, :cols] = jnp.sum(key_wide, axis=0, keepdims=True)
    stat[0, :, cols:] = jnp.where(lane == 0, query_sq, jnp.where(lane == 1, key_sq, 0.0))
    for k in range(1, n):
        send(stat.at[0], stat.at[k], st_s, st_r, {"parts": partner(k)})
    queries = spread_blocks(queryb, queryx, query_s, query_r)

    y_copies, numer = {}, {}

    def product(i):
        a, g = chunks[i]
        columns = pl.ds(g * width, width)
        if a == 0:
            first, second = keyb[c], keyx[0, 1 - c]
        else:
            first, second = keyx[1, c], keyx[1, 1 - c]
        whole = dot(first, val[c, :, columns]) + dot(second, val[1 - c, :, columns])
        tbuf[i] = whole.reshape(2, 4 * piece, width)
        ysend[i] = tbuf[i, 1 - y].astype(BF16)
        y_copies[i] = send(ysend.at[i], yrecv.at[i], y_s, y_r.at[i], {"parts": y_peer})

    def on_z(zz):
        return {"parts": zz * 4 + p % 4}

    z_copies, g_copies = {}, {}

    def z_send(i):
        y_copies[i].wait_recv()
        acc[i] = (tbuf[i, y] + yrecv[i].astype(F32)).reshape(4, piece, width)
        zsend[i] = acc[i].astype(BF16)
        near, mirror, far = range(3)
        z_copies[i] = [
            send(
                zsend.at[i, z_near],
                zrecv.at[i, near],
                z_s,
                z_r.at[i, 0],
                on_z(z_near),
            ),
            make(
                zsend.at[i, z_mirror],
                zrecv.at[i, mirror],
                z_s,
                z_r.at[i, 0],
                on_z(z_mirror),
            ),
        ]
        z_copies[i].append(
            send(
                zsend.at[i, z_far],
                zrecv.at[i, far],
                z_s,
                z_r.at[i, 1],
                on_z(jnp.where(edge, z_near, z_far)),
            )
        )

        @pl.when(edge)
        def _():
            z_copies[i][1].start()

    def z_combine(i):
        @pl.when(inner)
        def _():
            z_copies[i][2].wait_recv()
            zsend[i, z_mirror] = (acc[i, z_mirror] + zrecv[i, 2].astype(F32)).astype(BF16)
            z_copies[i][1].start()

    def pass_on(i, zz):
        place = kvl.at[i, spot_of(y, zz)]
        send(place, place, gy_s, gy_r.at[i], {"parts": y_peer})
        if chunks[i][0] == 1:
            g = chunks[i][1]
            target = kvx.at[g, spot_of(y, zz)]
            send(place, target, gx_s, gx_r.at[g], {"mp": other})
            send(place, target, gx_s, gx_r.at[g], {"parts": y_peer, "mp": other})

    def z_final(i):
        @pl.when(edge)
        def _():
            z_copies[i][2].wait_recv()

        wait_for(zrecv.at[i, pl.ds(0, 2)], z_r.at[i, 0])
        final = acc[i, z] + zrecv[i, 0].astype(F32) + zrecv[i, 1].astype(F32)
        final = final + jnp.where(edge, zrecv[i, 2].astype(F32), 0.0)
        place = kvl.at[i, spot_of(y, z)]
        place[...] = final.astype(BF16)
        g_copies[i] = [
            send(place, place, g_s, g_r.at[i, 0], on_z(z_near)),
            send(place, place, g_s, g_r.at[i, 1], on_z(z_mirror)),
            make(place, place, g_s, g_r.at[i, 2], on_z(z_far)),
        ]

        @pl.when(edge)
        def _():
            g_copies[i][2].start()

        pass_on(i, z)

    def z_gather_first(i):
        @pl.when(inner)
        def _():
            g_copies[i][1].wait_recv()
            place = kvl.at[i, spot_of(y, z_mirror)]
            send(place, place, g_s, g_r.at[i, 2], on_z(z_near))
            pass_on(i, z_mirror)

        g_copies[i][0].wait_recv()
        pass_on(i, z_near)

    def z_gather_last(i):
        @pl.when(edge)
        def _():
            g_copies[i][1].wait_recv()
            pass_on(i, z_mirror)

        g_copies[i][2].wait_recv()
        pass_on(i, z_far)

    num_copies = {}

    def store(place, core, side, g):
        target = kv_out.at[
            pl.ds(pl.multiple_of(core * half, half), half),
            pl.ds(pl.multiple_of(side * cols + g * width, width), width),
        ]
        pltpu.make_async_copy(place, target, osem).start()

    def y_gather(i):
        a, g = chunks[i]
        wait_for(yrecv.at[i], gy_r.at[i])
        if a == 0:
            send(
                kvl.at[i], kvs.at[g], gc_s, gc_r, {"parts": sibling}
            )
        block = kvl[i]
        if a == 0:
            numer[g] = [dot(queryb[c], block), dot(queryx[0, 1 - c], block)]
        else:
            nsend[g] = numer[g][1] + dot(queryx[1, 1 - c], block)
            num_copies[g] = send(
                nsend.at[g], nrecv.at[g], num_s, num_r.at[g], {"parts": sibling}
            )
            numer[g] = numer[g][0] + dot(queryx[1, c], block)

    def denominators():
        wait_for(stat.at[pl.ds(1, n - 1)], st_r)
        sums = stat[0]
        for k in range(1, n):
            sums = sums + stat[k]
        den[m, :rows, :] = jnp.broadcast_to(
            jnp.sum(query[...].astype(F32) * sums[:, :cols], axis=1, keepdims=True),
            (rows, 128),
        )
        den[m, rows:, :] = jnp.broadcast_to(sums[:, cols:], (8, 128))
        return send(den.at[m], den.at[m], den_sem.at[0], den_sem.at[1], {"mp": other})

    keys[2].wait_recv()
    values.wait_recv()
    early = [i for i, (a, _) in enumerate(chunks) if a == 0]
    for i in early:
        product(i)
    for copy in keys[:2]:
        copy.wait_recv()
    for i in range(len(chunks)):
        if i not in early:
            product(i)

    plan = []
    for i in range(len(chunks)):
        t = 3.0 + 1.3 * i + (0.4 if chunks[i][0] else 0.0)
        plan += [
            (t, z_send, i),
            (t + 2.1, z_combine, i),
            (t + 4.3, z_final, i),
            (t + 8.5, z_gather_first, i),
            (t + 11.0, z_gather_last, i),
            (t + 13.0, y_gather, i),
        ]
    queried = False
    for t, step, i in sorted(plan, key=lambda entry: entry[0]):
        if step is y_gather and not queried:
            queried = True
            den_swap = denominators()
            for copy in queries:
                copy.wait_recv()
        step(i)

    den_swap.wait_recv()
    square = den[0, rows : rows + 1, :] + den[1, rows : rows + 1, :]
    query_sq = jnp.sum(jnp.where(lane == 0, square, 0.0), axis=1, keepdims=True)
    key_sq = jnp.sum(jnp.where(lane == 1, square, 0.0), axis=1, keepdims=True)
    inverse = lax.rsqrt(query_sq) * lax.rsqrt(key_sq)
    denominator = den[0, :rows, 0:1] + den[1, :rows, 0:1]
    scale = 1.0 + denominator * inverse

    for i in early:
        store(kvl.at[i], c, m, chunks[i][1])
    wait_for(kvs, gc_r)
    for g in range(groups):
        store(kvs.at[g], 1 - c, m, g)
    for g in range(groups):
        columns = pl.ds(g * width, width)
        num_copies[g].wait_recv()
        result = (val[c, :, columns].astype(F32) + (numer[g] + nrecv[g]) * inverse) / scale
        out[:, columns] = jnp.where(live_mask, result, 0.0)
    last = []
    for g in range(groups):
        wait_for(kvx.at[g], gx_r.at[g])
        last.append(
            send(kvx.at[g], kvxs.at[g], gd_s, gd_r.at[g], {"parts": sibling})
        )
        store(kvx.at[g], c, other, g)
    for g in range(groups):
        last[g].wait_recv()
        store(kvxs.at[g], 1 - c, other, g)

    wait_for(outgoing.at[pl.ds(0, n - 1)], halo_s)
    wait_for(outgoing, fwd_s)
    wait_for(stat.at[pl.ds(1, n - 1)], st_s)
    wait_for(ysend, y_s)
    wait_for(zrecv, z_s)
    wait_for(zrecv, g_s)
    wait_for(yrecv, gy_s)
    wait_for(kvx, gx_s)
    wait_for(kvs, gc_s)
    wait_for(kvx, gd_s)
    wait_for(nsend, num_s)
    for copy in (swap_feats, swap, *keys, values, *queries, den_swap):
        copy.wait_send()
    wait_for(kv_out, osem)


def fused(
    feats, adj_local, adj_halo, w_graph, w_query, w_key, w_value, send_rows, send_count, live
):
    n = lax.axis_size("parts")
    rows, cols = feats.shape
    slots = send_rows.shape[2]
    depth = w_graph.shape[0]
    half, piece = cols // 2, cols // 16
    groups = 2
    width = cols // groups
    chunks = tuple((a, g) for a in range(2) for g in range(groups))
    count = len(chunks)
    vmem = pl.BlockSpec(memory_space=pltpu.VMEM)
    hbm = pl.BlockSpec(memory_space=pltpu.HBM)
    dma = pltpu.SemaphoreType.DMA
    place = functools.partial(pltpu.with_memory_space_constraint, memory_space=pltpu.HBM)
    gathered = (half, width)
    out, kv = pl.pallas_call(
        functools.partial(kernel, n, chunks),
        out_shape=(
            jax.ShapeDtypeStruct((rows, cols), F32),
            jax.ShapeDtypeStruct((cols, depth), BF16),
        ),
        in_specs=[hbm] * 5 + [pl.BlockSpec(memory_space=pltpu.SMEM)] + [hbm] * 4,
        out_specs=(vmem, pl.BlockSpec(memory_space=pl.ANY)),
        scratch_shapes=[
            pltpu.VMEM((2, rows, cols), BF16),
            pltpu.VMEM(adj_local.shape, BF16),
            pltpu.VMEM(adj_halo.shape, BF16),
            pltpu.VMEM((slots, n), jnp.int32),
            pltpu.VMEM((1, n), jnp.int32),
            pltpu.VMEM((4, depth, cols), BF16),
            pltpu.VMEM((n, slots, cols), BF16),
            pltpu.VMEM((2, n, slots, cols), BF16),
            pltpu.VMEM((2, rows, cols), BF16),
            pltpu.VMEM((2, rows, cols), BF16),
            pltpu.VMEM((2, rows, cols), BF16),
            pltpu.VMEM((rows, cols), BF16),
            pltpu.VMEM((2, half, rows), BF16),
            pltpu.VMEM((2, 2, half, rows), BF16),
            pltpu.VMEM((2, rows, half), BF16),
            pltpu.VMEM((2, 2, rows, half), BF16),
            pltpu.VMEM((count, 2, 4 * piece, width), F32),
            pltpu.VMEM((count, 4 * piece, width), BF16),
            pltpu.VMEM((count, 4 * piece, width), BF16),
            pltpu.VMEM((count, 4, piece, width), F32),
            pltpu.VMEM((count, 4, piece, width), BF16),
            pltpu.VMEM((count, 3, piece, width), BF16),
            pltpu.VMEM((count, *gathered), BF16),
            pltpu.VMEM((groups, *gathered), BF16),
            pltpu.VMEM((groups, *gathered), BF16),
            pltpu.VMEM((groups, *gathered), BF16),
            pltpu.VMEM((groups, rows, width), F32),
            pltpu.VMEM((groups, rows, width), F32),
            pltpu.VMEM((n, 1, cols + 128), F32),
            pltpu.VMEM((2, rows + 8, 128), F32),
            dma((5,)),
            dma((4,)),
            dma,
            dma((2,)),
            dma,
            dma((4,)),
            dma,
            dma,
            dma((2,)),
            dma((3,)),
            dma((3,)),
            dma((3,)),
            dma((3,)),
            dma((2,)),
            dma,
            dma((groups,)),
            dma,
            dma((count,)),
            dma,
            dma((count, 2)),
            dma,
            dma((count, 3)),
            dma,
            dma((count,)),
            dma,
            dma((groups,)),
            dma,
            dma,
            dma,
            dma((groups,)),
            dma,
            dma,
            dma((2,)),
        ],
        compiler_params=pltpu.CompilerParams(
            collective_id=0, has_side_effects=True, vmem_limit_bytes=24 * 1024 * 1024
        ),
    )(
        *(place(a) for a in (feats, adj_local, adj_halo, send_rows[0].T, send_count)),
        live,
        *(place(w) for w in (w_graph, w_query, w_key, w_value)),
    )
    return out, kv.astype(F32) / math.sqrt(n * rows)


def local(*args):
    n = lax.axis_size("parts")
    rows, cols = args[0].shape
    slots = args[7].shape[2]
    fits = (
        lax.axis_size("mp") == 2
        and n == 16
        and cols % 256 == 0
        and rows % 128 == 0
        and (n * slots) % 16 == 0
        and slots % 8 == 0
    )
    return fused(*args) if fits else plain(*args)


def solution(mesh):
    return jax.shard_map(
        local,
        mesh=mesh,
        in_specs=(
            P("parts", "mp"),
            P("parts", None),
            P("parts", None),
            P(None, "mp"),
            P(None, "mp"),
            P(None, "mp"),
            P(None, "mp"),
            P("parts", None, None),
            P("parts", None),
            P("parts"),
        ),
        out_specs=(P("parts", "mp"), P("mp", None)),
        check_vma=False,
    )
```

time: 55.8 us -> 52.7 us (0.944)
  Pallas kernels: 52 us -> 48.9 us
    pallas_call x1, Pallas kernels: 52 us -> 48.9 us  [fused(): pl.pallas_call(functools.partial(kernel, n, chunks), out_shape=(jax.Shape...]
where the time goes in v1:
time: 52.7 us; the launch traced here: 52.5 us
  Pallas kernels  48.9 us (93%)
  other arithmetic  1.6 us (3%)
  between operations  1.29 us (2%)
  local copies, waits for them, and re-layouts  0.7 us (1%)
    pallas_call x1, Pallas kernels, fused(): pl.pallas_call(functools.partial(kernel, n, chunks), out_shape=(jax.Shape...  48.9 us
    div x1, other arithmetic, fused(): return (out, kv.astype(F32) / math.sqrt(n * rows))  1.6 us

profile of v1, /device:TPU:0, one launch (start us, length us, event | category | flops | bytes accessed | tf_op | source)
XLA Modules:
  0.0 52.5 jit_solution(9285213347871650840)
XLA Ops:
  1.3 48.9 %shard_map.113 = (f32[128,512]{1,0:T(8,128)S(1)}, bf16[512,1024]{1,0:T(8,128)(2,1)S(1)}) custom-call(bf16[128,512]{1,0:T(8,128)(2,1)} %feats_in.1, bf16[128,128]{1,0:T(8,128)(2,1)} %adj_local_in.1, bf16[128,128]{1,0:T(8,128)(2,1)} %adj_halo_in.1, s32[8,16]{1,0:T(8,128)} %bitcast.3, s32[1,16]{1,0:T(1,128)} %send_count_in.1, s32[1]{0:T(128)S(6)} %copy.13.live, ...), custom_call_target="tpu_custom_call" | custom-call | tf_op jit(solution)/shard_map/pallas_call | solution.py:587
  50.2 1.6 %convert_multiply_fusion = f32[512,1024]{1,0:T(8,128)} fusion(bf16[512,1024]{1,0:T(8,128)(2,1)S(1)} %get-tuple-element.5), kind=kLoop, calls=%fused_computation | loop fusion | flops 1048576 | bytes 3145728 | tf_op jit(solution)/shard_map/div | solution.py:668
  51.8 0.7 %copy.14 = f32[128,512]{1,0:T(8,128)} copy(f32[128,512]{1,0:T(8,128)S(1)} %get-tuple-element.8) | data formatting | bytes 524288

commit v2 on v1

--- a/solution.py
+++ b/solution.py
@@ -166,14 +166,11 @@
     slots = outgoing.shape[1]
     total = n * slots
     half, piece = cols // 2, zrecv.shape[2]
-    width = zrecv.shape[3]
-    groups = cols // width
+    quarter = 4 * piece
 
     z_near = z + 1 - 2 * (z % 2)
     z_far = lax.rem(z + 2, 4)
     z_mirror = 3 - z
-    edge = jnp.logical_or(z == 0, z == 3)
-    inner = jnp.logical_not(edge)
 
     def spot_of(yy, zz):
         return pl.ds(pl.multiple_of((yy * 4 + zz) * piece, piece), piece)
@@ -341,143 +338,101 @@
         send(stat.at[0], stat.at[k], st_s, st_r, {"parts": partner(k)})
     queries = spread_blocks(queryb, queryx, query_s, query_r)
 
-    y_copies, numer = {}, {}
+    y_copies, g_copies, num_copies, numer = {}, {}, {}, {}
+    others = (z_near, z_far, z_mirror)
+
+    def span(i):
+        return pl.ds(chunks[i][1], chunks[i][2])
 
     def product(i):
-        a, g = chunks[i]
-        columns = pl.ds(g * width, width)
+        a, columns = chunks[i][0], span(i)
         if a == 0:
             first, second = keyb[c], keyx[0, 1 - c]
         else:
             first, second = keyx[1, c], keyx[1, 1 - c]
         whole = dot(first, val[c, :, columns]) + dot(second, val[1 - c, :, columns])
-        tbuf[i] = whole.reshape(2, 4 * piece, width)
-        ysend[i] = tbuf[i, 1 - y].astype(BF16)
-        y_copies[i] = send(ysend.at[i], yrecv.at[i], y_s, y_r.at[i], {"parts": y_peer})
+        tbuf[a, :, :, columns] = whole.reshape(2, quarter, chunks[i][2])
+        ysend[a, :, columns] = tbuf[a, 1 - y, :, columns].astype(BF16)
+        y_copies[i] = send(
+            ysend.at[a, :, columns], yrecv.at[a, :, columns], y_s, y_r.at[i], {"parts": y_peer}
+        )
 
     def on_z(zz):
         return {"parts": zz * 4 + p % 4}
 
-    z_copies, g_copies = {}, {}
-
     def z_send(i):
+        a, columns = chunks[i][0], span(i)
         y_copies[i].wait_recv()
-        acc[i] = (tbuf[i, y] + yrecv[i].astype(F32)).reshape(4, piece, width)
-        zsend[i] = acc[i].astype(BF16)
-        near, mirror, far = range(3)
-        z_copies[i] = [
+        whole = tbuf[a, y, :, columns] + yrecv[a, :, columns].astype(F32)
+        acc[a, :, :, columns] = whole.reshape(4, piece, chunks[i][2])
+        zsend[a, :, :, columns] = acc[a, :, :, columns].astype(BF16)
+        for k in (2, 1, 0):
             send(
-                zsend.at[i, z_near],
-                zrecv.at[i, near],
+                zsend.at[a, others[k], :, columns],
+                zrecv.at[a, k, :, columns],
                 z_s,
-                z_r.at[i, 0],
-                on_z(z_near),
-            ),
-            make(
-                zsend.at[i, z_mirror],
-                zrecv.at[i, mirror],
-                z_s,
-                z_r.at[i, 0],
-                on_z(z_mirror),
-            ),
-        ]
-        z_copies[i].append(
-            send(
-                zsend.at[i, z_far],
-                zrecv.at[i, far],
-                z_s,
-                z_r.at[i, 1],
-                on_z(jnp.where(edge, z_near, z_far)),
+                z_r.at[i],
+                on_z(others[k]),
             )
-        )
-
-        @pl.when(edge)
-        def _():
-            z_copies[i][1].start()
-
-    def z_combine(i):
-        @pl.when(inner)
-        def _():
-            z_copies[i][2].wait_recv()
-            zsend[i, z_mirror] = (acc[i, z_mirror] + zrecv[i, 2].astype(F32)).astype(BF16)
-            z_copies[i][1].start()
-
-    def pass_on(i, zz):
-        place = kvl.at[i, spot_of(y, zz)]
+
+    def pass_on(i, zz, direct):
+        a, columns = chunks[i][0], span(i)
+        place = kvl.at[a, spot_of(y, zz), columns]
         send(place, place, gy_s, gy_r.at[i], {"parts": y_peer})
-        if chunks[i][0] == 1:
-            g = chunks[i][1]
-            target = kvx.at[g, spot_of(y, zz)]
-            send(place, target, gx_s, gx_r.at[g], {"mp": other})
-            send(place, target, gx_s, gx_r.at[g], {"parts": y_peer, "mp": other})
+        if a == 1:
+            target = kvx.at[spot_of(y, zz), columns]
+            send(place, target, gx_s, gx_r.at[i], {"mp": other})
+            if direct:
+                send(place, target, gx_s, gx_r.at[i], {"parts": y_peer, "mp": other})
 
     def z_final(i):
-        @pl.when(edge)
-        def _():
-            z_copies[i][2].wait_recv()
-
-        wait_for(zrecv.at[i, pl.ds(0, 2)], z_r.at[i, 0])
-        final = acc[i, z] + zrecv[i, 0].astype(F32) + zrecv[i, 1].astype(F32)
-        final = final + jnp.where(edge, zrecv[i, 2].astype(F32), 0.0)
-        place = kvl.at[i, spot_of(y, z)]
+        a, columns = chunks[i][0], span(i)
+        wait_for(zrecv.at[a, :, :, columns], z_r.at[i])
+        final = acc[a, z, :, columns]
+        for k in range(3):
+            final = final + zrecv[a, k, :, columns].astype(F32)
+        place = kvl.at[a, spot_of(y, z), columns]
         place[...] = final.astype(BF16)
         g_copies[i] = [
-            send(place, place, g_s, g_r.at[i, 0], on_z(z_near)),
-            send(place, place, g_s, g_r.at[i, 1], on_z(z_mirror)),
-            make(place, place, g_s, g_r.at[i, 2], on_z(z_far)),
+            send(place, place, g_s, g_r.at[i, k], on_z(others[k])) for k in (2, 1, 0)
         ]
-
-        @pl.when(edge)
-        def _():
-            g_copies[i][2].start()
-
-        pass_on(i, z)
-
-    def z_gather_first(i):
-        @pl.when(inner)
-        def _():
-            g_copies[i][1].wait_recv()
-            place = kvl.at[i, spot_of(y, z_mirror)]
-            send(place, place, g_s, g_r.at[i, 2], on_z(z_near))
-            pass_on(i, z_mirror)
-
-        g_copies[i][0].wait_recv()
-        pass_on(i, z_near)
-
-    def z_gather_last(i):
-        @pl.when(edge)
-        def _():
-            g_copies[i][1].wait_recv()
-            pass_on(i, z_mirror)
-
-        g_copies[i][2].wait_recv()
-        pass_on(i, z_far)
-
-    num_copies = {}
-
-    def store(place, core, side, g):
+        pass_on(i, z, True)
+
+    def z_gather(i):
+        for k in range(3):
+            g_copies[i][2 - k].wait_recv()
+            pass_on(i, others[k], k == 0)
+
+    def store(place, core, side, columns):
         target = kv_out.at[
             pl.ds(pl.multiple_of(core * half, half), half),
-            pl.ds(pl.multiple_of(side * cols + g * width, width), width),
+            pl.ds(pl.multiple_of(side * cols + columns.start, 128), columns.size),
         ]
         pltpu.make_async_copy(place, target, osem).start()
 
     def y_gather(i):
-        a, g = chunks[i]
-        wait_for(yrecv.at[i], gy_r.at[i])
+        a, columns = chunks[i][0], span(i)
+        wait_for(yrecv.at[a, :, columns], gy_r.at[i])
         if a == 0:
             send(
-                kvl.at[i], kvs.at[g], gc_s, gc_r, {"parts": sibling}
+                kvl.at[0, :, columns], kvs.at[:, columns], gc_s, gc_r.at[i], {"parts": sibling}
             )
-        block = kvl[i]
-        if a == 0:
-            numer[g] = [dot(queryb[c], block), dot(queryx[0, 1 - c], block)]
-        else:
-            nsend[g] = numer[g][1] + dot(queryx[1, 1 - c], block)
-            num_copies[g] = send(
-                nsend.at[g], nrecv.at[g], num_s, num_r.at[g], {"parts": sibling}
+            return
+        for zz in others[1:]:
+            part = spot_of(1 - y, zz)
+            send(
+                kvl.at[1, part, columns],
+                kvx.at[part, columns],
+                gx_s,
+                gx_r.at[i],
+                {"mp": other},
             )
-            numer[g] = numer[g][0] + dot(queryx[1, c], block)
+        mine, theirs = kvl[0, :, columns], kvl[1, :, columns]
+        nsend[:, columns] = dot(queryx[0, 1 - c], mine) + dot(queryx[1, 1 - c], theirs)
+        num_copies[i] = send(
+            nsend.at[:, columns], nrecv.at[:, columns], num_s, num_r.at[i], {"parts": sibling}
+        )
+        numer[i] = dot(queryb[c], mine) + dot(queryx[1, c], theirs)
 
     def denominators():
         wait_for(stat.at[pl.ds(1, n - 1)], st_r)
@@ -493,7 +448,7 @@
 
     keys[2].wait_recv()
     values.wait_recv()
-    early = [i for i, (a, _) in enumerate(chunks) if a == 0]
+    early = [i for i, chunk in enumerate(chunks) if chunk[0] == 0]
     for i in early:
         product(i)
     for copy in keys[:2]:
@@ -502,25 +457,16 @@
         if i not in early:
             product(i)
 
-    plan = []
     for i in range(len(chunks)):
-        t = 3.0 + 1.3 * i + (0.4 if chunks[i][0] else 0.0)
-        plan += [
-            (t, z_send, i),
-            (t + 2.1, z_combine, i),
-            (t + 4.3, z_final, i),
-            (t + 8.5, z_gather_first, i),
-            (t + 11.0, z_gather_last, i),
-            (t + 13.0, y_gather, i),
-        ]
-    queried = False
-    for t, step, i in sorted(plan, key=lambda entry: entry[0]):
-        if step is y_gather and not queried:
-            queried = True
-            den_swap = denominators()
-            for copy in queries:
-                copy.wait_recv()
-        step(i)
+        z_send(i)
+    den_swap = denominators()
+    for step in (z_final, z_gather):
+        for i in range(len(chunks)):
+            step(i)
+    for copy in queries:
+        copy.wait_recv()
+    for i in range(len(chunks)):
+        y_gather(i)
 
     den_swap.wait_recv()
     square = den[0, rows : rows + 1, :] + den[1, rows : rows + 1, :]
@@ -530,26 +476,26 @@
     denominator = den[0, :rows, 0:1] + den[1, :rows, 0:1]
     scale = 1.0 + denominator * inverse
 
+    late = [i for i in range(len(chunks)) if i not in early]
     for i in early:
-        store(kvl.at[i], c, m, chunks[i][1])
-    wait_for(kvs, gc_r)
-    for g in range(groups):
-        store(kvs.at[g], 1 - c, m, g)
-    for g in range(groups):
-        columns = pl.ds(g * width, width)
-        num_copies[g].wait_recv()
-        result = (val[c, :, columns].astype(F32) + (numer[g] + nrecv[g]) * inverse) / scale
-        out[:, columns] = jnp.where(live_mask, result, 0.0)
-    last = []
-    for g in range(groups):
-        wait_for(kvx.at[g], gx_r.at[g])
-        last.append(
-            send(kvx.at[g], kvxs.at[g], gd_s, gd_r.at[g], {"parts": sibling})
-        )
-        store(kvx.at[g], c, other, g)
-    for g in range(groups):
-        last[g].wait_recv()
-        store(kvxs.at[g], 1 - c, other, g)
+        store(kvl.at[0, :, span(i)], c, m, span(i))
+    for i in early:
+        wait_for(kvs.at[:, span(i)], gc_r.at[i])
+        store(kvs.at[:, span(i)], 1 - c, m, span(i))
+    for i in late:
+        columns = span(i)
+        num_copies[i].wait_recv()
+        result = val[c, :, columns].astype(F32) + (numer[i] + nrecv[:, columns]) * inverse
+        out[:, columns] = jnp.where(live_mask, result / scale, 0.0)
+    last = {}
+    for i in late:
+        place = kvx.at[:, span(i)]
+        wait_for(place, gx_r.at[i])
+        last[i] = send(place, kvxs.at[:, span(i)], gd_s, gd_r.at[i], {"parts": sibling})
+        store(place, c, other, span(i))
+    for i in late:
+        last[i].wait_recv()
+        store(kvxs.at[:, span(i)], 1 - c, other, span(i))
 
     wait_for(outgoing.at[pl.ds(0, n - 1)], halo_s)
     wait_for(outgoing, fwd_s)
@@ -575,15 +521,13 @@
     slots = send_rows.shape[2]
     depth = w_graph.shape[0]
     half, piece = cols // 2, cols // 16
-    groups = 2
-    width = cols // groups
-    chunks = tuple((a, g) for a in range(2) for g in range(groups))
+    quarter = half // 2
+    chunks = ((0, 0, half), (0, half, half), (1, 0, half), (1, half, quarter), (1, half + quarter, quarter))
     count = len(chunks)
     vmem = pl.BlockSpec(memory_space=pltpu.VMEM)
     hbm = pl.BlockSpec(memory_space=pltpu.HBM)
     dma = pltpu.SemaphoreType.DMA
     place = functools.partial(pltpu.with_memory_space_constraint, memory_space=pltpu.HBM)
-    gathered = (half, width)
     out, kv = pl.pallas_call(
         functools.partial(kernel, n, chunks),
         out_shape=(
@@ -609,18 +553,18 @@
             pltpu.VMEM((2, 2, half, rows), BF16),
             pltpu.VMEM((2, rows, half), BF16),
             pltpu.VMEM((2, 2, rows, half), BF16),
-            pltpu.VMEM((count, 2, 4 * piece, width), F32),
-            pltpu.VMEM((count, 4 * piece, width), BF16),
-            pltpu.VMEM((count, 4 * piece, width), BF16),
-            pltpu.VMEM((count, 4, piece, width), F32),
-            pltpu.VMEM((count, 4, piece, width), BF16),
-            pltpu.VMEM((count, 3, piece, width), BF16),
-            pltpu.VMEM((count, *gathered), BF16),
-            pltpu.VMEM((groups, *gathered), BF16),
-            pltpu.VMEM((groups, *gathered), BF16),
-            pltpu.VMEM((groups, *gathered), BF16),
-            pltpu.VMEM((groups, rows, width), F32),
-            pltpu.VMEM((groups, rows, width), F32),
+            pltpu.VMEM((2, 2, 4 * piece, cols), F32),
+            pltpu.VMEM((2, 4 * piece, cols), BF16),
+            pltpu.VMEM((2, 4 * piece, cols), BF16),
+            pltpu.VMEM((2, 4, piece, cols), F32),
+            pltpu.VMEM((2, 4, piece, cols), BF16),
+            pltpu.VMEM((2, 3, piece, cols), BF16),
+            pltpu.VMEM((2, half, cols), BF16),
+            pltpu.VMEM((half, cols), BF16),
+            pltpu.VMEM((half, cols), BF16),
+            pltpu.VMEM((half, cols), BF16),
+            pltpu.VMEM((rows, cols), F32),
+            pltpu.VMEM((rows, cols), F32),
             pltpu.VMEM((n, 1, cols + 128), F32),
             pltpu.VMEM((2, rows + 8, 128), F32),
             dma((5,)),
@@ -638,21 +582,21 @@
             dma((3,)),
             dma((2,)),
             dma,
-            dma((groups,)),
-            dma,
             dma((count,)),
             dma,
-            dma((count, 2)),
+            dma((count,)),
+            dma,
+            dma((count,)),
             dma,
             dma((count, 3)),
             dma,
             dma((count,)),
             dma,
-            dma((groups,)),
-            dma,
-            dma,
-            dma,
-            dma((groups,)),
+            dma((count,)),
+            dma,
+            dma((count,)),
+            dma,
+            dma((count,)),
             dma,
             dma,
             dma((2,)),
@@ -675,7 +619,7 @@
     fits = (
         lax.axis_size("mp") == 2
         and n == 16
-        and cols % 256 == 0
+        and cols % 512 == 0
         and rows % 128 == 0
         and (n * slots) % 16 == 0
         and slots % 8 == 0

time: 52.7 us -> 51 us (0.968)
  Pallas kernels: 48.9 us -> 47.2 us
    pallas_call x1, Pallas kernels: 48.9 us -> 47.2 us  [fused(): pl.pallas_call(functools.partial(kernel, n, chunks), out_shape=(jax.Shape...]
where the time goes in v2:
time: 51 us; the launch traced here: 50.8 us
  Pallas kernels  47.2 us (93%)
  other arithmetic  1.6 us (3%)
  between operations  1.29 us (3%)
  local copies, waits for them, and re-layouts  0.7 us (1%)
    pallas_call x1, Pallas kernels, fused(): pl.pallas_call(functools.partial(kernel, n, chunks), out_shape=(jax.Shape...  47.2 us
    div x1, other arithmetic, fused(): return (out, kv.astype(F32) / math.sqrt(n * rows))  1.6 us

profile of v2, /device:TPU:0, one launch (start us, length us, event | category | flops | bytes accessed | tf_op | source)
XLA Modules:
  0.0 50.8 jit_solution(13602075033281455418)
XLA Ops:
  1.3 47.2 %shard_map.113 = (f32[128,512]{1,0:T(8,128)S(1)}, bf16[512,1024]{1,0:T(8,128)(2,1)S(1)}) custom-call(bf16[128,512]{1,0:T(8,128)(2,1)} %feats_in.1, bf16[128,128]{1,0:T(8,128)(2,1)} %adj_local_in.1, bf16[128,128]{1,0:T(8,128)(2,1)} %adj_halo_in.1, s32[8,16]{1,0:T(8,128)} %bitcast.3, s32[1,16]{1,0:T(1,128)} %send_count_in.1, s32[1]{0:T(128)S(6)} %copy.13.live, ...), custom_call_target="tpu_custom_call" | custom-call | tf_op jit(solution)/shard_map/pallas_call | solution.py:531
  48.5 1.6 %convert_multiply_fusion = f32[512,1024]{1,0:T(8,128)} fusion(bf16[512,1024]{1,0:T(8,128)(2,1)S(1)} %get-tuple-element.5), kind=kLoop, calls=%fused_computation | loop fusion | flops 1048576 | bytes 3145728 | tf_op jit(solution)/shard_map/div | solution.py:612
  50.1 0.7 %copy.14 = f32[128,512]{1,0:T(8,128)} copy(f32[128,512]{1,0:T(8,128)S(1)} %get-tuple-element.8) | data formatting | bytes 524288

commit v3 on v2

--- a/solution.py
+++ b/solution.py
@@ -206,11 +206,6 @@
         load = pltpu.make_async_copy(source, place, isem.at[i])
         load.start()
         inputs.append(load)
-    loads = []
-    for i, w in enumerate((wg, wk, wv, wq)):
-        load = pltpu.make_async_copy(w, wbuf.at[i], wsem.at[i])
-        load.start()
-        loads.append(load)
 
     barrier = pltpu.get_barrier_semaphore()
     for d in range(1, n):
@@ -224,6 +219,11 @@
 
     for load in inputs:
         load.wait()
+    loads = []
+    for i, w in enumerate((wg, wk, wv, wq)):
+        load = pltpu.make_async_copy(w, wbuf.at[i], wsem.at[i])
+        load.start()
+        loads.append(load)
 
     owner = lax.broadcasted_iota(jnp.int32, (total, n), 0) // slots
     is_owner = owner == lax.broadcasted_iota(jnp.int32, (total, n), 1)
@@ -262,15 +262,14 @@
         to = partner(k)
         send(outgoing.at[to], incoming.at[m, p], halo_s, halo_r.at[k // 4], {"parts": to})
     swap_feats = send(feats.at[m], feats.at[m], feat_sem.at[0], feat_sem.at[1], {"mp": other})
-    send(outgoing.at[p], incoming.at[m, p], fwd_s, fwd_r, {"mp": other})
     incoming[m, p] = outgoing[p]
     local_mine = dot(adj_local[...], feats[m])
     for kz in range(4):
         members = range(max(1, 4 * kz), 4 * kz + 4)
         wait_for(outgoing.at[pl.ds(0, len(members))], halo_r.at[kz])
-        for k in members:
-            block = incoming.at[m, partner(k)]
-            send(block, block, fwd_s, fwd_r, {"mp": other})
+        first = pl.multiple_of((z, z_near, z_far, z_mirror)[kz] * 4, 4)
+        block = incoming.at[m, pl.ds(first, 4)]
+        send(block, block, fwd_s, fwd_r, {"mp": other})
 
     def convolve(side, local_sum):
         arrived = incoming[side].astype(F32).reshape(total, cols).astype(BF16)

time: 51 us -> 49.9 us (0.978)
  Pallas kernels: 47.2 us -> 46.1 us
    pallas_call x1, Pallas kernels: 47.2 us -> 46.1 us  [fused(): pl.pallas_call(functools.partial(kernel, n, chunks), out_shape=(jax.Shape...]
where the time goes in v3:
time: 49.9 us; the launch traced here: 49.7 us
  Pallas kernels  46.1 us (92%)
  other arithmetic  1.6 us (3%)
  between operations  1.29 us (3%)
  local copies, waits for them, and re-layouts  0.7 us (1%)
    pallas_call x1, Pallas kernels, fused(): pl.pallas_call(functools.partial(kernel, n, chunks), out_shape=(jax.Shape...  46.1 us
    div x1, other arithmetic, fused(): return (out, kv.astype(F32) / math.sqrt(n * rows))  1.6 us

profile of v3, /device:TPU:0, one launch (start us, length us, event | category | flops | bytes accessed | tf_op | source)
XLA Modules:
  0.0 49.7 jit_solution(2972653460485241173)
XLA Ops:
  1.3 46.1 %shard_map.113 = (f32[128,512]{1,0:T(8,128)S(1)}, bf16[512,1024]{1,0:T(8,128)(2,1)S(1)}) custom-call(bf16[128,512]{1,0:T(8,128)(2,1)} %feats_in.1, bf16[128,128]{1,0:T(8,128)(2,1)} %adj_local_in.1, bf16[128,128]{1,0:T(8,128)(2,1)} %adj_halo_in.1, s32[8,16]{1,0:T(8,128)} %bitcast.3, s32[1,16]{1,0:T(1,128)} %send_count_in.1, s32[1]{0:T(128)S(6)} %copy.13.live, ...), custom_call_target="tpu_custom_call" | custom-call | tf_op jit(solution)/shard_map/pallas_call | solution.py:530
  47.4 1.6 %convert_multiply_fusion = f32[512,1024]{1,0:T(8,128)} fusion(bf16[512,1024]{1,0:T(8,128)(2,1)S(1)} %get-tuple-element.5), kind=kLoop, calls=%fused_computation | loop fusion | flops 1048576 | bytes 3145728 | tf_op jit(solution)/shard_map/div | solution.py:611
  49.0 0.7 %copy.14 = f32[128,512]{1,0:T(8,128)} copy(f32[128,512]{1,0:T(8,128)S(1)} %get-tuple-element.8) | data formatting | bytes 524288
